TPU v7x, 32 devices: a whole 2x2x4 slice. The times are simulated.
32 devices in a mesh: row: 4 (over y, core), blk: 8 (over z, x).
Axes of the slice: x: 2, y: 2, z: 4, core: 2. Of those that a mesh axis runs over, the one named last changes fastest.
Arguments:
- matrix: float32 [16384, 2048], P('row', 'blk'), may hold values from -6 to 6
Outputs:
- rotated: float32 [16384, 2048], P('row', 'blk')
- off_measure: float32 [2], replicated
All inputs are finite; a program needn't handle non-finite values.
Results may differ from a plain program's by a relative error of at most 0.00012.
Values sent between devices are 32-bit elements; how exact they have to be, the bound alone decides.
A program may use at most 64 MiB of HBM per device.

v0:
```python
import jax
import jax.numpy as jnp
from jax import lax
from jax.sharding import PartitionSpec as P

STEPS = 2
NS_ITERS = 4


HIGH = lax.Precision.HIGHEST


def shifted(value, axis, steps):
    count = lax.axis_size(axis)
    pairs = [(source, (source + steps) % count) for source in range(count)]
    return lax.ppermute(value, axis, pairs)


def gram_of(first_part, second_part):
    return lax.dot_general(first_part, second_part, (((0,), (0,)), ((), ())), precision=HIGH)


def matmul(first_part, second_part):
    return jnp.dot(first_part, second_part, precision=HIGH)


def inverse_root(square, bound_scale):
    identity = jnp.eye(square.shape[0], dtype=jnp.float32)
    current = square / bound_scale
    result = identity
    for count_index in range(NS_ITERS):
        factor = 1.5 * identity - 0.5 * matmul(result, current)
        current = matmul(current, factor)
        result = matmul(factor, result)
    return result / jnp.sqrt(bound_scale)


def on_device(matrix):
    width = matrix.shape[1] // 2
    left_block = matrix[:, :width]
    right_block = matrix[:, width:]
    identity = jnp.eye(width, dtype=jnp.float32)
    total_list = []
    for step_index in range(STEPS):
        cross_gram, first_norms, second_norms = lax.psum(
            (
                gram_of(left_block, right_block),
                jnp.sum(left_block * left_block, axis=0),
                jnp.sum(right_block * right_block, axis=0),
            ),
            "row",
        )
        cosines = cross_gram * lax.rsqrt(first_norms)[:, None] * lax.rsqrt(second_norms)[None, :]
        local_sum = jnp.sum(cosines * cosines)
        total_list.append(lax.psum(local_sum, "blk"))
        coupling = 0.5 * cosines
        bound_scale = 1.0 + jnp.sum(coupling * coupling)
        first_root = inverse_root(identity + matmul(coupling, coupling.T), bound_scale)
        second_root = inverse_root(identity + matmul(coupling.T, coupling), bound_scale)
        first_moves = step_index % 2 == 0
        if first_moves:
            own_block, other_block = (left_block, right_block)
            move_mix, move_root = (-coupling.T, first_root)
            stay_mix, stay_root = (coupling, second_root)
        else:
            own_block, other_block = (right_block, left_block)
            move_mix, move_root = (coupling, second_root)
            stay_mix, stay_root = (-coupling.T, first_root)
        staying = matmul(other_block + matmul(own_block, stay_mix), stay_root)
        moving = matmul(own_block + matmul(other_block, move_mix), move_root)
        arrived = shifted(moving, "blk", 1)
        if first_moves:
            left_block, right_block = (arrived, staying)
        else:
            left_block, right_block = (staying, arrived)
    totals = jnp.stack(total_list)
    off_measure = totals / float(lax.axis_size("blk"))
    rotated = jnp.concatenate([left_block, right_block], axis=1)
    return (rotated, off_measure)


def solution(mesh):
    return jax.shard_map(
        on_device,
        mesh=mesh,
        in_specs=(P("row", "blk"),),
        out_specs=(P("row", "blk"), P()),
        check_vma=False,
    )
```

profile of v0, /device:TPU:0, one launch (start us, length us, event | category | flops | bytes accessed | tf_op | source)
XLA Modules:
  0.0 244.0 jit_solution(7852412305849070871)
XLA Ops:
  7.2 6.3 %fusion.3 = f32[128,128]{1,0:T(8,128)} fusion(f32[4096,256]{1,0:T(8,128)} %param.1), kind=kOutput, calls=%fused_computation.12 | convolution fusion | flops 805306368 | bytes 4259840 | tf_op jit(solution)/shard_map/dot_general | solution.py:20
  13.6 2.8 %multiply_reduce_fusion.3 = (f32[128]{0:T(128)S(1)}, f32[128]{0:T(128)S(1)}) fusion(f32[4096,256]{1,0:T(8,128)} %param.1), kind=kLoop, calls=%fused_computation.10 | loop fusion | flops 2096896 | bytes 4195328 | tf_op jit(solution)/shard_map/reduce_sum | solution.py:48
  16.4 8.4 %all-reduce.2 = (f32[128]{0:T(128)S(1)}, f32[128]{0:T(128)S(1)}) all-reduce(f32[128]{0:T(128)S(1)} %get-tuple-element.5, f32[128]{0:T(128)S(1)} %get-tuple-element.4), channel_id=1, replica_groups=mesh['row'=4,'blk'=8] {'row'}, use_global_device_ids=true, to_apply=%region_4.0 | all-reduce | flops 256 | bytes 2048 | tf_op jit(solution)/shard_map/psum | solution.py:45
  24.8 23.2 %all-reduce.6.cloned.1.call-done = f32[128,128]{1,0:T(8,128)} async-done(((f32[128,128]{1,0:T(8,128)}), f32[128,128]{1,0:T(8,128)}) %all-reduce.6.cloned.1.call-update) | async-done | bytes 65552 | tf_op jit(solution)/shard_map/psum | solution.py:45
  47.9 1.6 multiply_reduce_fusion.5
  55.7 4.1 %fusion.1 = f32[4096,128]{1,0:T(8,128)S(1)} fusion(f32[4096,256]{1,0:T(8,128)} %param.1, f32[128,128]{1,0:T(8,128)S(1)} %copy-done.4, f32[128]{0:T(128)S(1)} %rsqrt.13, f32[128]{0:T(128)S(1)} %rsqrt.12), kind=kOutput, calls=%fused_computation.5 | convolution fusion | flops 805896192 | bytes 6358016 | tf_op jit(solution)/shard_map/dot_general | solution.py:24
  59.8 1.9 fusion.48
  61.7 1.7 collective-permute-start
  65.1 2.1 fusion
  67.1 1.8 multiply_reduce_fusion
  69.0 41.7 %collective-permute-done = f32[4096,128]{1,0:T(8,128)S(1)} collective-permute-done((f32[4096,128]{1,0:T(8,128)S(1)}, f32[4096,128]{1,0:T(8,128)S(1)}, u32[]{:S(2)}, u32[]{:S(2)}) %collective-permute-start) | collective-permute-done | bytes 2097184 | tf_op jit(solution)/shard_map/ppermute | solution.py:16
  110.7 4.1 %fusion.54 = f32[128,128]{1,0:T(8,128)} fusion(f32[4096,128]{1,0:T(8,128)S(1)} %collective-permute-done, f32[4096,128]{1,0:T(8,128)S(1)} %get-tuple-element.17), kind=kOutput, calls=%fused_computation.87 | convolution fusion | flops 805306368 | bytes 4259840 | tf_op jit(solution)/shard_map/dot_general | solution.py:20
  115.4 5.9 %all-reduce.1 = (f32[128]{0:T(128)S(1)}, f32[128]{0:T(128)S(1)}) all-reduce(f32[128]{0:T(128)S(1)} %get-tuple-element.16, f32[128]{0:T(128)S(1)} %multiply_reduce_fusion.1), channel_id=1, replica_groups=mesh['row'=4,'blk'=8] {'row'}, use_global_device_ids=true, to_apply=%region_10.0 | all-reduce | flops 256 | bytes 2048 | tf_op jit(solution)/shard_map/psum | solution.py:45
  121.3 23.0 %all-reduce.8.cloned.1.call-done = f32[128,128]{1,0:T(8,128)} async-done(((f32[128,128]{1,0:T(8,128)}), f32[128,128]{1,0:T(8,128)}) %all-reduce.8.cloned.1.call-update) | async-done | bytes 65552 | tf_op jit(solution)/shard_map/psum | solution.py:45
  144.3 1.6 multiply_reduce_fusion.4
  152.6 1.9 convolution_add_fusion
  154.5 3.4 %fusion.66 = f32[4096,128]{0,1:T(8,128)} fusion(f32[4096,128]{1,0:T(8,128)S(1)} %convolution_add_fusion, f32[128,128]{1,0:T(8,128)S(1)} %convolution_divide_fusion), kind=kOutput, calls=%fused_computation.99 | convolution fusion | flops 805306368 | bytes 4259840 | tf_op jit(solution)/shard_map/dot_general | solution.py:24
  157.9 1.5 collective-permute-start.1
  159.4 59.6 %all-reduce = (f32[1]{0:T(128)}, f32[1]{0:T(128)}) all-reduce(f32[1]{0:T(128)} %bitcast.3, f32[1]{0:T(128)} %bitcast.2), channel_id=1, replica_groups=mesh['row'=4,'blk'=8] {'blk'}, use_global_device_ids=true, to_apply=%region_15.0 | all-reduce | flops 2 | bytes 16 | tf_op jit(solution)/shard_map/psum | solution.py:55
  218.9 1.8 maximum_multiply_fusion
  222.0 3.6 %convolution_add_fusion.1 = f32[4096,128]{1,0:T(8,128)S(1)} fusion(f32[4096,128]{1,0:T(8,128)S(1)} %collective-permute-done, f32[4096,128]{1,0:T(8,128)} %copy-done.1, f32[128,128]{1,0:T(8,128)S(1)} %copy-done.3, f32[128]{0:T(128)S(1)} %rsqrt.15, f32[128]{0:T(128)S(1)} %rsqrt.14), kind=kOutput, calls=%fused_computation.1 | convolution fusion | flops 805896192 | bytes 6358016 | tf_op jit(solution)/shard_map/dot_general | solution.py:24
  225.6 2.0 fusion.60
  227.6 4.0 %pad_maximum_fusion = f32[4096,256]{0,1:T(8,128)} fusion(f32[4096,128]{0,1:T(8,128)} %collective-permute-done.1, f32[4096,128]{0,1:T(8,128)S(1)} %fusion.60), kind=kLoop, calls=%fused_computation.6 | loop fusion | flops 1048576 | bytes 8388608 | tf_op jit(solution)/shard_map/concatenate | solution.py:78
  231.6 5.6 %copy.4 = f32[4096,256]{1,0:T(8,128)} copy(f32[4096,256]{0,1:T(8,128)} %pad_maximum_fusion) | data formatting | bytes 8388608
  (68 shorter events, 14.7 us)
Async XLA Ops:
  7.2 40.8 %all-reduce.6.cloned.1.call-start = ((), (), s32[]{:S(2)}) async-start(), calls=%async_computation | async-start | bytes 131072 | tf_op jit(solution)/shard_map/psum | solution.py:45
  13.5 130.8 %all-reduce.8.cloned.1.call-start = ((), (), s32[]{:S(2)}) async-start(), calls=%async_computation.1 | async-start | bytes 131072 | tf_op jit(solution)/shard_map/psum | solution.py:45
  47.9 7.7 %copy-start.4 = (f32[128,128]{1,0:T(8,128)S(1)}, f32[128,128]{1,0:T(8,128)}, u32[]{:S(2)}) copy-start(f32[128,128]{1,0:T(8,128)} %all-reduce.6.cloned.1.call-done) | copy-start | bytes 196612
  59.8 5.3 %copy-start = (f32[4096,256]{1,0:T(8,128)S(1)}, f32[4096,256]{1,0:T(8,128)}, u32[]{:S(2)}) copy-start(f32[4096,256]{1,0:T(8,128)} %param.1) | copy-start | bytes 12582916
  61.7 49.0 %collective-permute-start = (f32[4096,128]{1,0:T(8,128)S(1)}, f32[4096,128]{1,0:T(8,128)S(1)}, u32[]{:S(2)}, u32[]{:S(2)}) collective-permute-start(f32[4096,128]{1,0:T(8,128)S(1)} %fusion.48), channel_id=1, source_target_pairs={{0,1},{1,2},{2,3},{3,4},{4,5},{5,6},{6,7},{7,0},{8,9},{9,10},{10,1... | collective-permute-start | bytes 6291464 | tf_op jit(solution)/shard_map/ppermute | solution.py:16
  69.0 41.7 %copy-start.1 = (f32[4096,128]{1,0:T(8,128)}, f32[4096,128]{1,0:T(8,128)S(1)}, u32[]{:S(2)}) copy-start(f32[4096,128]{1,0:T(8,128)S(1)} %get-tuple-element.17) | copy-start | bytes 6291460
  144.3 8.3 %copy-start.3 = (f32[128,128]{1,0:T(8,128)S(1)}, f32[128,128]{1,0:T(8,128)}, u32[]{:S(2)}) copy-start(f32[128,128]{1,0:T(8,128)} %all-reduce.8.cloned.1.call-done) | copy-start | bytes 196612
  148.4 4.1 %copy-start.2 = (f32[4096,128]{1,0:T(8,128)S(1)}, f32[4096,128]{1,0:T(8,128)}, u32[]{:S(2)}) copy-start(f32[4096,128]{1,0:T(8,128)} %copy-done.1) | copy-start | bytes 6291460
  157.9 69.7 %collective-permute-start.1 = (f32[4096,128]{0,1:T(8,128)}, f32[4096,128]{0,1:T(8,128)}, u32[]{:S(2)}, u32[]{:S(2)}) collective-permute-start(f32[4096,128]{0,1:T(8,128)} %fusion.66), channel_id=1, source_target_pairs={{0,1},{1,2},{2,3},{3,4},{4,5},{5,6},{6,7},{7,0},{8,9},{9,10},{10,1... | collective-permute-start | bytes 6291464 | tf_op jit(solution)/shard_map/ppermute | solution.py:16
Sparse Core Ops, SparseCore 0:
  13.7 34.2 all-reduce.5
  114.9 29.3 all-reduce.7
where the time goes:
time: 245 us; the launch traced here: 244 us
  waiting for transfers between devices  87.9 us (36%)
  blocking collectives  73.9 us (30%)
  matrix products  45.1 us (18%)
  between operations  15.9 us (6%)
  other arithmetic  12.4 us (5%)
  local copies, waits for them, and re-layouts  5.63 us (2%)
  starting transfers between devices  3.25 us (1%)
    psum x1, blocking collectives, on_device(): total_list.append(lax.psum(local_sum, 'blk'))  59.6 us
    psum x2, waiting for transfers between devices, on_device(): lax.psum((gram_of(left_block, right_block), jnp.sum(left_block * left_blo...  46.2 us
    ppermute x2, waiting for transfers between devices, shifted(): return lax.ppermute(value, axis, pairs)  41.7 us
    dot_general x56, matrix products, matmul(): return jnp.dot(first_part, second_part, precision=HIGH)  34.7 us
    psum x2, blocking collectives, on_device(): lax.psum((gram_of(left_block, right_block), jnp.sum(left_block * left_blo...  14.3 us
    dot_general x2, matrix products, gram_of(): lax.dot_general(first_part, second_part, (((0,), (0,)), ((), ())), precis...  10.4 us
    unnamed x11, local copies, waits for them, and re-layouts  5.62 us
  transfers between devices with their start and end apart: 4, of which 3 were waited for; matrix products, arithmetic and copies ran while one was open for 7% of the time, Pallas kernels for 0%

commit v1 on v0

v1 whole, which is shorter than its diff:
```python
import functools

import jax
import jax.numpy as jnp
from jax import lax
from jax.experimental import pallas as pl
from jax.experimental.pallas import tpu as pltpu
from jax.sharding import PartitionSpec as P

STEPS = 2
NS_ITERS = 4
MESH = pl.DeviceIdType.MESH
F32 = jnp.float32
BF16 = jnp.bfloat16


def split(value):
    high = value.astype(BF16)
    return high, (value - high.astype(F32)).astype(BF16)


def dot(a, b):
    return jnp.dot(a, b, preferred_element_type=F32)


def product(a, b):
    ah, al = split(a)
    bh, bl = split(b)
    width = b.shape[1]
    both = dot(
        jnp.concatenate([ah, al], axis=1),
        jnp.concatenate(
            [
                jnp.concatenate([bh, bl], axis=1),
                jnp.concatenate([bh, jnp.zeros_like(bl)], axis=1),
            ],
            axis=0,
        ),
    )
    return both[:, :width] + both[:, width:]


def mixing(cosines):
    width = cosines.shape[0]
    rows = lax.broadcasted_iota(jnp.int32, (width, width), 0)
    columns = lax.broadcasted_iota(jnp.int32, (width, width), 1)
    identity = jnp.where(rows == columns, 1.0, 0.0).astype(F32)
    coupling = 0.5 * cosines
    flipped = coupling.T
    scale = 1.0 + jnp.sum(coupling * coupling, keepdims=True)
    shrink = 1.0 / scale
    current = [
        (identity + product(coupling, flipped)) * shrink,
        (identity + product(flipped, coupling)) * shrink,
    ]
    result = [None, None]
    for count in range(NS_ITERS):
        for side in range(2):
            y, z = current[side], result[side]
            inner = y if z is None else product(z, y)
            factor = 1.5 * identity - 0.5 * inner
            if count < NS_ITERS - 1:
                current[side] = product(y, factor)
            result[side] = factor if z is None else product(factor, z)
    root = 1.0 / jnp.sqrt(scale)
    first, second = result[0] * root, result[1] * root
    return (
        jnp.concatenate([first, product(coupling, second)], axis=1),
        jnp.concatenate([-product(flipped, first), second], axis=1),
    )


def kernel(
    row_count, blk_count, chunk, gram_chunk,
    x_hbm, out_hbm, off_ref,
    xv, move0, stay0, come0, move1, stay1, acc, norms, gath, weights, measure, mgath,
    load_sem, send0, recv0, send1, recv1, out_sem, gsend, grecv, msend, mrecv,
):
    rows, both = x_hbm.shape
    width = both // 2
    chunks = rows // chunk
    row, blk = lax.axis_index("row"), lax.axis_index("blk")
    after = lax.rem(blk + 1, blk_count)

    barrier = pltpu.get_barrier_semaphore()
    for k in range(1, row_count):
        pl.semaphore_signal(
            barrier, inc=1, device_id={"row": lax.rem(row + k, row_count)}, device_id_type=MESH
        )

    def greet(k, carry):
        pl.semaphore_signal(
            barrier, inc=1, device_id={"blk": lax.rem(blk + k, blk_count)}, device_id_type=MESH
        )
        return carry

    lax.fori_loop(1, blk_count, greet, 0)

    def at(i, size):
        return pl.ds(pl.multiple_of(i * size, size), size)

    def load(i):
        return pltpu.make_async_copy(
            x_hbm.at[at(i, gram_chunk)], xv.at[at(i, gram_chunk)], load_sem.at[i]
        )

    def start_load(i, carry):
        load(i).start()
        return carry

    lax.fori_loop(0, rows // gram_chunk, start_load, 0)

    def add_gram(left, right):
        lh, ll = split(left)
        rh, rl = split(right)
        acc[...] += lax.dot_general(
            jnp.concatenate([lh, ll], axis=1),
            jnp.concatenate([rh, rl], axis=1),
            (((0,), (0,)), ((), ())),
            preferred_element_type=F32,
        )
        norms[0:8] += jnp.sum((left * left).reshape(-1, 8, width), axis=0)
        norms[8:16] += jnp.sum((right * right).reshape(-1, 8, width), axis=0)

    def clear():
        acc[...] = jnp.zeros_like(acc)
        norms[...] = jnp.zeros_like(norms)

    def exchange(step, peer_of):
        def copy(owner, peer, k):
            return pltpu.make_async_remote_copy(
                src_ref=gath.at[step, owner],
                dst_ref=gath.at[step, owner],
                send_sem=gsend.at[step, k],
                recv_sem=grecv.at[step, owner],
                device_id={"row": peer},
                device_id_type=MESH,
            )

        gath[step, row, 0:width] = (
            acc[:width, :width] + acc[:width, width:] + acc[width:, :width]
        ) + acc[width:, width:]
        first = jnp.sum(norms[0:8], axis=0, keepdims=True)
        second = jnp.sum(norms[8:16], axis=0, keepdims=True)
        gath[step, row, width:width + 8] = jnp.broadcast_to(first, (8, width))
        gath[step, row, width + 8:width + 16] = jnp.broadcast_to(second, (8, width))
        if step == 0:
            pl.semaphore_wait(barrier, row_count + blk_count - 2)
        for k in range(1, row_count):
            copy(row, lax.rem(row + k, row_count), k).start()
        for k in range(1, row_count):
            peer = lax.rem(row + k, row_count)
            copy(peer, peer, k).wait_recv()
        total = gath[step, 0]
        for r in range(1, row_count):
            total = total + gath[step, r]
        for k in range(1, row_count):
            copy(row, lax.rem(row + k, row_count), k).wait_send()
        cross = total[:width]
        first = lax.rsqrt(jnp.broadcast_to(total[width:width + 1], (width, width))).T
        second = lax.rsqrt(jnp.broadcast_to(total[width + 8:width + 9], (width, width)))
        cosines = cross * first * second
        measure[step:step + 1] = jnp.broadcast_to(
            jnp.sum(cosines * cosines, keepdims=True), (1, width)
        )
        top, bottom = mixing(cosines)
        high, low = split(top)
        weights[0, :width] = high
        weights[1, :width] = low
        high, low = split(bottom)
        weights[0, width:] = high
        weights[1, width:] = low

    def transform(left, right):
        lh, ll = split(left)
        rh, rl = split(right)
        high = jnp.concatenate([lh, rh], axis=1)
        low = jnp.concatenate([ll, rl], axis=1)
        return dot(high, weights[0]) + (dot(high, weights[1]) + dot(low, weights[0]))

    def first_move(i):
        return pltpu.make_async_remote_copy(
            src_ref=move0.at[at(i, chunk)], dst_ref=come0.at[at(i, chunk)],
            send_sem=send0.at[i], recv_sem=recv0.at[i],
            device_id={"blk": after}, device_id_type=MESH,
        )

    def second_move(i):
        return pltpu.make_async_remote_copy(
            src_ref=move1.at[at(i, chunk)], dst_ref=out_hbm.at[at(i, chunk), pl.ds(width, width)],
            send_sem=send1.at[i], recv_sem=recv1.at[i],
            device_id={"blk": after}, device_id_type=MESH,
        )

    def store(i):
        return pltpu.make_async_copy(
            stay1.at[at(i, chunk)], out_hbm.at[at(i, chunk), pl.ds(0, width)], out_sem.at[i]
        )

    def message(owner, peer):
        return pltpu.make_async_remote_copy(
            src_ref=mgath.at[owner], dst_ref=mgath.at[owner],
            send_sem=msend.at[peer], recv_sem=mrecv.at[owner],
            device_id={"blk": peer}, device_id_type=MESH,
        )

    clear()

    def gram0(i, carry):
        load(i).wait()
        part = at(i, gram_chunk)
        add_gram(xv[part, 0:width], xv[part, width:both])
        return carry

    lax.fori_loop(0, rows // gram_chunk, gram0, 0)
    measure[...] = jnp.zeros_like(measure)
    exchange(0, None)

    def turn0(i, carry):
        part = at(i, chunk)
        mixed = transform(xv[part, 0:width], xv[part, width:both])
        move0[part] = mixed[:, :width]
        stay0[part] = mixed[:, width:]

        @pl.when(i > 0)
        def _():
            first_move(i - 1).start()

        return carry

    lax.fori_loop(0, chunks, turn0, 0)
    first_move(chunks - 1).start()

    clear()

    def gram1(i, carry):
        first_move(i).wait_recv()
        part = at(i, chunk)
        add_gram(come0[part], stay0[part])
        return carry

    lax.fori_loop(0, chunks, gram1, 0)
    exchange(1, None)

    def turn1(i, carry):
        part = at(i, chunk)
        mixed = transform(come0[part], stay0[part])
        stay1[part] = mixed[:, :width]
        move1[part] = mixed[:, width:]

        @pl.when(i > 0)
        def _():
            second_move(i - 1).start()
            store(i - 1).start()

        return carry

    lax.fori_loop(0, chunks, turn1, 0)
    second_move(chunks - 1).start()
    store(chunks - 1).start()

    mgath[blk] = measure[...]

    def tell(k, carry):
        message(blk, lax.rem(blk + k, blk_count)).start()
        return carry

    lax.fori_loop(1, blk_count, tell, 0)

    def hear(k, carry):
        peer = lax.rem(blk + k, blk_count)
        message(peer, peer).wait_recv()
        return carry

    lax.fori_loop(1, blk_count, hear, 0)
    means = jnp.sum(mgath[...], axis=0) / float(blk_count)
    for step in range(STEPS):
        off_ref[step] = jnp.max(means[step:step + 1])

    def finish(i, carry):
        first_move(i).wait_send()
        store(i).wait()
        second_move(i).wait_send()
        second_move(i).wait_recv()
        return carry

    lax.fori_loop(0, chunks, finish, 0)

    def told(k, carry):
        message(blk, lax.rem(blk + k, blk_count)).wait_send()
        return carry

    lax.fori_loop(1, blk_count, told, 0)


def on_device(row_count, blk_count, matrix):
    rows, both = matrix.shape
    width = both // 2
    chunk = rows // 16
    gram_chunk = rows // 8
    dma = pltpu.SemaphoreType.DMA
    block = pltpu.VMEM((rows, width), F32)
    return pl.pallas_call(
        functools.partial(kernel, row_count, blk_count, chunk, gram_chunk),
        out_shape=(
            jax.ShapeDtypeStruct((rows, both), F32),
            jax.ShapeDtypeStruct((STEPS,), F32),
        ),
        in_specs=[pl.BlockSpec(memory_space=pl.ANY)],
        out_specs=(
            pl.BlockSpec(memory_space=pl.ANY),
            pl.BlockSpec(memory_space=pltpu.SMEM),
        ),
        scratch_shapes=[
            pltpu.VMEM((rows, both), F32),
            block, block, block, block, block,
            pltpu.VMEM((both, both), F32),
            pltpu.VMEM((16, width), F32),
            pltpu.VMEM((STEPS, row_count, width + 16, width), F32),
            pltpu.VMEM((2, both, both), BF16),
            pltpu.VMEM((8, width), F32),
            pltpu.VMEM((blk_count, 8, width), F32),
            dma((rows // gram_chunk,)),
            dma((16,)), dma((16,)), dma((16,)), dma((16,)), dma((16,)),
            dma((STEPS, row_count)), dma((STEPS, row_count)),
            dma((blk_count,)), dma((blk_count,)),
        ],
        compiler_params=pltpu.CompilerParams(
            collective_id=0, has_side_effects=True, vmem_limit_bytes=40 * 1024 * 1024
        ),
    )(matrix)


def solution(mesh):
    return jax.shard_map(
        functools.partial(on_device, mesh.shape["row"], mesh.shape["blk"]),
        mesh=mesh,
        in_specs=(P("row", "blk"),),
        out_specs=(P("row", "blk"), P()),
        check_vma=False,
    )
```

time: 245 us -> 123 us (0.50)
  Pallas kernels: 0 us -> 118 us
  waiting for transfers between devices: 87.9 us -> 0 us
  blocking collectives: 73.9 us -> 0 us
  matrix products: 45.1 us -> 0 us
  between operations: 15.9 us -> 0.65 us
  other arithmetic: 12.4 us -> 0 us
  starting transfers between devices: 3.25 us -> 0 us
    pallas_call x0 -> x1, Pallas kernels: none -> 118 us  [on_device(): pl.pallas_call(functools.partial(kernel, row_count, blk_count, chunk, gra...]
    psum x3 -> x0, blocking collectives: 73.9 us -> none  [the longest x1 59.6 us: on_device(): total_list.append(lax.psum(local_sum, 'blk'))]
    psum x2 -> x0, waiting for transfers between devices: 46.2 us -> none  [on_device(): lax.psum((gram_of(left_block, right_block), jnp.sum(left_block * left_blo...]
    dot_general x58 -> x0, matrix products: 45.1 us -> none  [the longest x56 34.7 us: matmul(): return jnp.dot(first_part, second_part, precision=HIGH)]
    ppermute x2 -> x0, waiting for transfers between devices: 41.7 us -> none  [shifted(): return lax.ppermute(value, axis, pairs)]
    reduce_sum x4 -> x0, other arithmetic: 6.58 us -> none  [the longest x2 3.33 us: on_device(): jnp.sum(left_block * left_block, axis=0)]
    concatenate x1 -> x0, other arithmetic: 3.97 us -> none  [on_device(): rotated = jnp.concatenate([left_block, right_block], axis=1)]
    ppermute x2 -> x0, starting transfers between devices: 3.17 us -> none  [shifted(): return lax.ppermute(value, axis, pairs)]
  transfers between devices with their start and end apart: 4 -> 0, of which waited for: 3 -> 0; matrix products, arithmetic and copies ran while one was open for 7% -> 0% of each run, Pallas kernels for 0% -> 0%
where the time goes in v1:
time: 123 us
  Pallas kernels  118 us (96%)
  local copies, waits for them, and re-layouts  4.71 us (4%)
    pallas_call x1, Pallas kernels, on_device(): pl.pallas_call(functools.partial(kernel, row_count, blk_count, chunk, gra...  118 us
    unnamed x4, local copies, waits for them, and re-layouts  4.71 us

profile of v1, /device:TPU:0, one launch (start us, length us, event | category | flops | bytes accessed | tf_op | source)
XLA Modules:
  0.0 123.3 jit_solution(6903028237596885623)
XLA Ops:
  0.6 0.0 copy-start
  0.6 2.2 %copy-done = f32[4096,256]{1,0:T(8,128)S(1)} copy-done((f32[4096,256]{1,0:T(8,128)S(1)}, f32[4096,256]{1,0:T(8,128)}, u32[]{:S(2)}) %copy-start) | copy-done | bytes 4194328
  2.8 118.0 %shard_map.30 = (f32[4096,256]{1,0:T(8,128)S(1)}, f32[2]{0:T(128)S(1)}) custom-call(f32[4096,256]{1,0:T(8,128)S(1)} %copy-done), custom_call_target="tpu_custom_call" | custom-call | tf_op jit(solution)/shard_map/pallas_call | solution.py:303
  120.8 2.0 %copy.5 = f32[4096,256]{1,0:T(8,128)} copy(f32[4096,256]{1,0:T(8,128)S(1)} %get-tuple-element.4) | data formatting | bytes 8388608
  122.8 0.5 copy.6
Async XLA Ops:
  0.6 2.2 %copy-start = (f32[4096,256]{1,0:T(8,128)S(1)}, f32[4096,256]{1,0:T(8,128)}, u32[]{:S(2)}) copy-start(f32[4096,256]{1,0:T(8,128)} %x_hbm.1) | copy-start | bytes 12582916

commit v2 on v1

--- a/solution.py
+++ b/solution.py
@@ -71,16 +71,19 @@
 
 
 def kernel(
-    row_count, blk_count, chunk, gram_chunk,
-    x_hbm, out_hbm, off_ref,
-    xv, move0, stay0, come0, move1, stay1, acc, norms, gath, weights, measure, mgath,
-    load_sem, send0, recv0, send1, recv1, out_sem, gsend, grecv, msend, mrecv,
+    row_count, blk_count, chunk, gram_chunk, early,
+    x_hbm, out_ref, off_ref,
+    xv, move0, stay0, come0, move1, raw, rest, skip,
+    acc, norms, gath, weights, coses, cosin, measure, mgath,
+    load_sem, send0, recv0, send1, recv1, gsend, grecv, msend, mrecv, esend, erecv,
 ):
     rows, both = x_hbm.shape
     width = both // 2
     chunks = rows // chunk
     row, blk = lax.axis_index("row"), lax.axis_index("blk")
     after = lax.rem(blk + 1, blk_count)
+    second = lax.rem(blk + 2, blk_count)
+    early_rows = pl.ds(0, early * chunk)
 
     barrier = pltpu.get_barrier_semaphore()
     for k in range(1, row_count):
@@ -109,6 +112,19 @@
         return carry
 
     lax.fori_loop(0, rows // gram_chunk, start_load, 0)
+
+    def ahead(source, target, k, peer):
+        return pltpu.make_async_remote_copy(
+            src_ref=source, dst_ref=target, send_sem=esend.at[k], recv_sem=erecv.at[k],
+            device_id={"blk": peer}, device_id_type=MESH,
+        )
+
+    raw_move = ahead(x_hbm.at[early_rows], raw, 0, after)
+    skip_move = ahead(move0.at[early_rows], skip, 1, second)
+    cos_moves = [ahead(coses.at[s], cosin.at[s], 2 + s, after) for s in range(STEPS)]
+
+    pl.semaphore_wait(barrier, row_count + blk_count - 2)
+    raw_move.start()
 
     def add_gram(left, right):
         lh, ll = split(left)
@@ -126,7 +142,16 @@
         acc[...] = jnp.zeros_like(acc)
         norms[...] = jnp.zeros_like(norms)
 
-    def exchange(step, peer_of):
+    def mix(slot, cosines):
+        top, bottom = mixing(cosines)
+        high, low = split(top)
+        weights[slot, 0, :width] = high
+        weights[slot, 1, :width] = low
+        high, low = split(bottom)
+        weights[slot, 0, width:] = high
+        weights[slot, 1, width:] = low
+
+    def exchange(step):
         def copy(owner, peer, k):
             return pltpu.make_async_remote_copy(
                 src_ref=gath.at[step, owner],
@@ -144,8 +169,6 @@
         second = jnp.sum(norms[8:16], axis=0, keepdims=True)
         gath[step, row, width:width + 8] = jnp.broadcast_to(first, (8, width))
         gath[step, row, width + 8:width + 16] = jnp.broadcast_to(second, (8, width))
-        if step == 0:
-            pl.semaphore_wait(barrier, row_count + blk_count - 2)
         for k in range(1, row_count):
             copy(row, lax.rem(row + k, row_count), k).start()
         for k in range(1, row_count):
@@ -163,20 +186,17 @@
         measure[step:step + 1] = jnp.broadcast_to(
             jnp.sum(cosines * cosines, keepdims=True), (1, width)
         )
-        top, bottom = mixing(cosines)
-        high, low = split(top)
-        weights[0, :width] = high
-        weights[1, :width] = low
-        high, low = split(bottom)
-        weights[0, width:] = high
-        weights[1, width:] = low
-
-    def transform(left, right):
+        coses[step] = cosines
+        mix(0, cosines)
+        cos_moves[step].start()
+
+    def transform(slot, left, right):
         lh, ll = split(left)
         rh, rl = split(right)
         high = jnp.concatenate([lh, rh], axis=1)
         low = jnp.concatenate([ll, rl], axis=1)
-        return dot(high, weights[0]) + (dot(high, weights[1]) + dot(low, weights[0]))
+        own, fine = weights[slot, 0], weights[slot, 1]
+        return dot(high, own) + (dot(high, fine) + dot(low, own))
 
     def first_move(i):
         return pltpu.make_async_remote_copy(
@@ -187,14 +207,9 @@
 
     def second_move(i):
         return pltpu.make_async_remote_copy(
-            src_ref=move1.at[at(i, chunk)], dst_ref=out_hbm.at[at(i, chunk), pl.ds(width, width)],
+            src_ref=move1.at[at(i, chunk)], dst_ref=out_ref.at[at(i, chunk), pl.ds(width, width)],
             send_sem=send1.at[i], recv_sem=recv1.at[i],
             device_id={"blk": after}, device_id_type=MESH,
-        )
-
-    def store(i):
-        return pltpu.make_async_copy(
-            stay1.at[at(i, chunk)], out_hbm.at[at(i, chunk), pl.ds(0, width)], out_sem.at[i]
         )
 
     def message(owner, peer):
@@ -214,24 +229,46 @@
 
     lax.fori_loop(0, rows // gram_chunk, gram0, 0)
     measure[...] = jnp.zeros_like(measure)
-    exchange(0, None)
+    exchange(0)
 
     def turn0(i, carry):
         part = at(i, chunk)
-        mixed = transform(xv[part, 0:width], xv[part, width:both])
+        mixed = transform(0, xv[part, 0:width], xv[part, width:both])
         move0[part] = mixed[:, :width]
         stay0[part] = mixed[:, width:]
 
-        @pl.when(i > 0)
+        @pl.when(i > early)
         def _():
             first_move(i - 1).start()
 
         return carry
 
-    lax.fori_loop(0, chunks, turn0, 0)
+    lax.fori_loop(early, chunks, turn0, 0)
     first_move(chunks - 1).start()
 
+    def own0(i, carry):
+        part = at(i, chunk)
+        mixed = transform(0, xv[part, 0:width], xv[part, width:both])
+        move0[part] = mixed[:, :width]
+        stay0[part] = mixed[:, width:]
+        return carry
+
+    lax.fori_loop(0, early, own0, 0)
+
+    cos_moves[0].wait_recv()
+    mix(1, cosin[0])
+    raw_move.wait_recv()
     clear()
+
+    def early0(i, carry):
+        part = at(i, chunk)
+        mixed = transform(1, raw[part, 0:width], raw[part, width:both])
+        come0[part] = mixed[:, :width]
+        rest[part] = mixed[:, width:]
+        add_gram(mixed[:, :width], stay0[part])
+        return carry
+
+    lax.fori_loop(0, early, early0, 0)
 
     def gram1(i, carry):
         first_move(i).wait_recv()
@@ -239,25 +276,41 @@
         add_gram(come0[part], stay0[part])
         return carry
 
-    lax.fori_loop(0, chunks, gram1, 0)
-    exchange(1, None)
+    lax.fori_loop(early, chunks, gram1, 0)
+    skip_move.start()
+    exchange(1)
 
     def turn1(i, carry):
         part = at(i, chunk)
-        mixed = transform(come0[part], stay0[part])
-        stay1[part] = mixed[:, :width]
+        mixed = transform(0, come0[part], stay0[part])
+        out_ref[part, 0:width] = mixed[:, :width]
         move1[part] = mixed[:, width:]
 
-        @pl.when(i > 0)
+        @pl.when(i > early)
         def _():
             second_move(i - 1).start()
-            store(i - 1).start()
-
-        return carry
-
-    lax.fori_loop(0, chunks, turn1, 0)
+
+        return carry
+
+    lax.fori_loop(early, chunks, turn1, 0)
     second_move(chunks - 1).start()
-    store(chunks - 1).start()
+
+    def own1(i, carry):
+        part = at(i, chunk)
+        out_ref[part, 0:width] = transform(0, come0[part], stay0[part])[:, :width]
+        return carry
+
+    lax.fori_loop(0, early, own1, 0)
+    cos_moves[1].wait_recv()
+    mix(1, cosin[1])
+    skip_move.wait_recv()
+
+    def early1(i, carry):
+        part = at(i, chunk)
+        out_ref[part, width:both] = transform(1, skip[part], rest[part])[:, width:]
+        return carry
+
+    lax.fori_loop(0, early, early1, 0)
 
     mgath[blk] = measure[...]
 
@@ -279,12 +332,15 @@
 
     def finish(i, carry):
         first_move(i).wait_send()
-        store(i).wait()
         second_move(i).wait_send()
         second_move(i).wait_recv()
         return carry
 
-    lax.fori_loop(0, chunks, finish, 0)
+    lax.fori_loop(early, chunks, finish, 0)
+    raw_move.wait_send()
+    skip_move.wait_send()
+    for cos_move in cos_moves:
+        cos_move.wait_send()
 
     def told(k, carry):
         message(blk, lax.rem(blk + k, blk_count)).wait_send()
@@ -296,34 +352,41 @@
 def on_device(row_count, blk_count, matrix):
     rows, both = matrix.shape
     width = both // 2
-    chunk = rows // 16
+    chunks, early = 16, 2
+    chunk = rows // chunks
     gram_chunk = rows // 8
     dma = pltpu.SemaphoreType.DMA
     block = pltpu.VMEM((rows, width), F32)
+    some = pltpu.VMEM((early * chunk, width), F32)
     return pl.pallas_call(
-        functools.partial(kernel, row_count, blk_count, chunk, gram_chunk),
+        functools.partial(kernel, row_count, blk_count, chunk, gram_chunk, early),
         out_shape=(
             jax.ShapeDtypeStruct((rows, both), F32),
             jax.ShapeDtypeStruct((STEPS,), F32),
         ),
-        in_specs=[pl.BlockSpec(memory_space=pl.ANY)],
+        in_specs=[pl.BlockSpec(memory_space=pltpu.HBM)],
         out_specs=(
-            pl.BlockSpec(memory_space=pl.ANY),
+            pl.BlockSpec(memory_space=pltpu.VMEM),
             pl.BlockSpec(memory_space=pltpu.SMEM),
         ),
         scratch_shapes=[
             pltpu.VMEM((rows, both), F32),
-            block, block, block, block, block,
+            block, block, block, block,
+            pltpu.VMEM((early * chunk, both), F32),
+            some, some,
             pltpu.VMEM((both, both), F32),
             pltpu.VMEM((16, width), F32),
             pltpu.VMEM((STEPS, row_count, width + 16, width), F32),
-            pltpu.VMEM((2, both, both), BF16),
+            pltpu.VMEM((2, 2, both, both), BF16),
+            pltpu.VMEM((STEPS, width, width), F32),
+            pltpu.VMEM((STEPS, width, width), F32),
             pltpu.VMEM((8, width), F32),
             pltpu.VMEM((blk_count, 8, width), F32),
             dma((rows // gram_chunk,)),
-            dma((16,)), dma((16,)), dma((16,)), dma((16,)), dma((16,)),
+            dma((chunks,)), dma((chunks,)), dma((chunks,)), dma((chunks,)),
             dma((STEPS, row_count)), dma((STEPS, row_count)),
             dma((blk_count,)), dma((blk_count,)),
+            dma((2 + STEPS,)), dma((2 + STEPS,)),
         ],
         compiler_params=pltpu.CompilerParams(
             collective_id=0, has_side_effects=True, vmem_limit_bytes=40 * 1024 * 1024

time: 123 us -> 116 us (0.943)
  Pallas kernels: 118 us -> 111 us
    pallas_call x1, Pallas kernels: 118 us -> 111 us  [on_device(): pl.pallas_call(functools.partial(kernel, row_count, blk_count, chunk, gra...]
where the time goes in v2:
time: 116 us
  Pallas kernels  111 us (96%)
  local copies, waits for them, and re-layouts  4.71 us (4%)
    pallas_call x1, Pallas kernels, on_device(): pl.pallas_call(functools.partial(kernel, row_count, blk_count, chunk, gra...  111 us
    unnamed x4, local copies, waits for them, and re-layouts  4.71 us

profile of v2, /device:TPU:0, one launch (start us, length us, event | category | flops | bytes accessed | tf_op | source)
XLA Modules:
  0.0 116.2 jit_solution(3989047664153159667)
XLA Ops:
  0.6 0.0 copy-start
  0.6 2.2 %copy-done = f32[4096,256]{1,0:T(8,128)S(1)} copy-done((f32[4096,256]{1,0:T(8,128)S(1)}, f32[4096,256]{1,0:T(8,128)}, u32[]{:S(2)}) %copy-start) | copy-done | bytes 4194328
  2.8 110.8 %shard_map.30 = (f32[4096,256]{1,0:T(8,128)S(1)}, f32[2]{0:T(128)S(1)}) custom-call(f32[4096,256]{1,0:T(8,128)S(1)} %copy-done), custom_call_target="tpu_custom_call" | custom-call | tf_op jit(solution)/shard_map/pallas_call | solution.py:361
  113.6 2.0 %copy.5 = f32[4096,256]{1,0:T(8,128)} copy(f32[4096,256]{1,0:T(8,128)S(1)} %get-tuple-element.4) | data formatting | bytes 8388608
  115.7 0.5 copy.6
Async XLA Ops:
  0.6 2.2 %copy-start = (f32[4096,256]{1,0:T(8,128)S(1)}, f32[4096,256]{1,0:T(8,128)}, u32[]{:S(2)}) copy-start(f32[4096,256]{1,0:T(8,128)} %x_hbm.1) | copy-start | bytes 12582916

commit v3 on v2

--- a/solution.py
+++ b/solution.py
@@ -352,7 +352,7 @@
 def on_device(row_count, blk_count, matrix):
     rows, both = matrix.shape
     width = both // 2
-    chunks, early = 16, 2
+    chunks, early = 16, 3
     chunk = rows // chunks
     gram_chunk = rows // 8
     dma = pltpu.SemaphoreType.DMA
@@ -389,7 +389,7 @@
             dma((2 + STEPS,)), dma((2 + STEPS,)),
         ],
         compiler_params=pltpu.CompilerParams(
-            collective_id=0, has_side_effects=True, vmem_limit_bytes=40 * 1024 * 1024
+            collective_id=0, has_side_effects=True, vmem_limit_bytes=48 * 1024 * 1024
         ),
     )(matrix)
 

time: 116 us -> 117 us (level)
  local copies, waits for them, and re-layouts: 4.71 us -> 2.53 us
  Pallas kernels: 111 us -> 113 us
    pallas_call x1, Pallas kernels: 111 us -> 113 us  [on_device(): pl.pallas_call(functools.partial(kernel, row_count, blk_count, chunk, gra...]
    unnamed x4 -> x2, local copies, waits for them, and re-layouts: 4.71 us -> 2.53 us
where the time goes in v3:
time: 117 us; the launch traced here: 116 us
  Pallas kernels  113 us (97%)
  local copies, waits for them, and re-layouts  2.53 us (2%)
    pallas_call x1, Pallas kernels, on_device(): pl.pallas_call(functools.partial(kernel, row_count, blk_count, chunk, gra...  113 us
    unnamed x2, local copies, waits for them, and re-layouts  2.53 us

profile of v3, /device:TPU:0, one launch (start us, length us, event | category | flops | bytes accessed | tf_op | source)
XLA Modules:
  0.0 116.4 jit_solution(4549972564064808830)
XLA Ops:
  0.6 113.3 %shard_map.30 = (f32[4096,256]{1,0:T(8,128)S(1)}, f32[2]{0:T(128)S(1)}) custom-call(f32[4096,256]{1,0:T(8,128)} %x_hbm.1), custom_call_target="tpu_custom_call" | custom-call | tf_op jit(solution)/shard_map/pallas_call | solution.py:361
  113.9 2.0 %copy.5 = f32[4096,256]{1,0:T(8,128)} copy(f32[4096,256]{1,0:T(8,128)S(1)} %get-tuple-element.4) | data formatting | bytes 8388608
  115.9 0.5 copy.6

commit v4 on v3

--- a/solution.py
+++ b/solution.py
@@ -71,9 +71,9 @@
 
 
 def kernel(
-    row_count, blk_count, chunk, gram_chunk, early,
+    row_count, blk_count, chunk, gram_chunk, early, given,
     x_hbm, out_ref, off_ref,
-    xv, move0, stay0, come0, move1, raw, rest, skip,
+    xv, move0, stay0, come0, move1, raw, rest, skip, hold,
     acc, norms, gath, weights, coses, cosin, measure, mgath,
     load_sem, send0, recv0, send1, recv1, gsend, grecv, msend, mrecv, esend, erecv,
 ):
@@ -83,7 +83,10 @@
     row, blk = lax.axis_index("row"), lax.axis_index("blk")
     after = lax.rem(blk + 1, blk_count)
     second = lax.rem(blk + 2, blk_count)
+    odd = lax.rem(blk, 2) == 1
+    below = lax.rem(blk + blk_count - 1, blk_count)
     early_rows = pl.ds(0, early * chunk)
+    given_rows = pl.ds(early * chunk, (given - early) * chunk)
 
     barrier = pltpu.get_barrier_semaphore()
     for k in range(1, row_count):
@@ -113,14 +116,18 @@
 
     lax.fori_loop(0, rows // gram_chunk, start_load, 0)
 
-    def ahead(source, target, k, peer):
+    def ahead(source, target, k, peer, sender=None):
+        sender = k if sender is None else sender
         return pltpu.make_async_remote_copy(
-            src_ref=source, dst_ref=target, send_sem=esend.at[k], recv_sem=erecv.at[k],
+            src_ref=source, dst_ref=target, send_sem=esend.at[sender], recv_sem=erecv.at[k],
             device_id={"blk": peer}, device_id_type=MESH,
         )
 
     raw_move = ahead(x_hbm.at[early_rows], raw, 0, after)
-    skip_move = ahead(move0.at[early_rows], skip, 1, second)
+    skip_move = ahead(move0.at[pl.ds(0, given * chunk)], skip, 1, second)
+    give_move = ahead(stay0.at[given_rows], rest.at[given_rows], 2 + STEPS, after)
+    hold_move = ahead(stay0.at[given_rows], hold, 3 + STEPS, below)
+    pass_move = ahead(hold, rest.at[given_rows], 2 + STEPS, second, 4 + STEPS)
     cos_moves = [ahead(coses.at[s], cosin.at[s], 2 + s, after) for s in range(STEPS)]
 
     pl.semaphore_wait(barrier, row_count + blk_count - 2)
@@ -187,8 +194,8 @@
             jnp.sum(cosines * cosines, keepdims=True), (1, width)
         )
         coses[step] = cosines
+        cos_moves[step].start()
         mix(0, cosines)
-        cos_moves[step].start()
 
     def transform(slot, left, right):
         lh, ll = split(left)
@@ -278,6 +285,15 @@
 
     lax.fori_loop(early, chunks, gram1, 0)
     skip_move.start()
+
+    @pl.when(odd)
+    def _():
+        hold_move.start()
+
+    @pl.when(jnp.logical_not(odd))
+    def _():
+        give_move.start()
+
     exchange(1)
 
     def turn1(i, carry):
@@ -286,31 +302,38 @@
         out_ref[part, 0:width] = mixed[:, :width]
         move1[part] = mixed[:, width:]
 
-        @pl.when(i > early)
+        @pl.when(i > given)
         def _():
             second_move(i - 1).start()
 
         return carry
 
-    lax.fori_loop(early, chunks, turn1, 0)
+    lax.fori_loop(given, chunks, turn1, 0)
     second_move(chunks - 1).start()
 
+    @pl.when(jnp.logical_not(odd))
+    def _():
+        hold_move.wait_recv()
+        pass_move.start()
+
+
     def own1(i, carry):
         part = at(i, chunk)
         out_ref[part, 0:width] = transform(0, come0[part], stay0[part])[:, :width]
         return carry
 
-    lax.fori_loop(0, early, own1, 0)
+    lax.fori_loop(0, given, own1, 0)
     cos_moves[1].wait_recv()
     mix(1, cosin[1])
     skip_move.wait_recv()
+    give_move.wait_recv()
 
     def early1(i, carry):
         part = at(i, chunk)
         out_ref[part, width:both] = transform(1, skip[part], rest[part])[:, width:]
         return carry
 
-    lax.fori_loop(0, early, early1, 0)
+    lax.fori_loop(0, given, early1, 0)
 
     mgath[blk] = measure[...]
 
@@ -331,12 +354,26 @@
         off_ref[step] = jnp.max(means[step:step + 1])
 
     def finish(i, carry):
-        first_move(i).wait_send()
         second_move(i).wait_send()
         second_move(i).wait_recv()
         return carry
 
-    lax.fori_loop(early, chunks, finish, 0)
+    def sent(i, carry):
+        first_move(i).wait_send()
+        return carry
+
+    lax.fori_loop(early, chunks, sent, 0)
+    lax.fori_loop(given, chunks, finish, 0)
+
+    @pl.when(odd)
+    def _():
+        hold_move.wait_send()
+
+    @pl.when(jnp.logical_not(odd))
+    def _():
+        give_move.wait_send()
+        pass_move.wait_send()
+
     raw_move.wait_send()
     skip_move.wait_send()
     for cos_move in cos_moves:
@@ -352,14 +389,14 @@
 def on_device(row_count, blk_count, matrix):
     rows, both = matrix.shape
     width = both // 2
-    chunks, early = 16, 3
+    chunks, early, given = 16, 2, 4
     chunk = rows // chunks
     gram_chunk = rows // 8
     dma = pltpu.SemaphoreType.DMA
     block = pltpu.VMEM((rows, width), F32)
-    some = pltpu.VMEM((early * chunk, width), F32)
+    some = pltpu.VMEM((given * chunk, width), F32)
     return pl.pallas_call(
-        functools.partial(kernel, row_count, blk_count, chunk, gram_chunk, early),
+        functools.partial(kernel, row_count, blk_count, chunk, gram_chunk, early, given),
         out_shape=(
             jax.ShapeDtypeStruct((rows, both), F32),
             jax.ShapeDtypeStruct((STEPS,), F32),
@@ -374,6 +411,7 @@
             block, block, block, block,
             pltpu.VMEM((early * chunk, both), F32),
             some, some,
+            pltpu.VMEM(((given - early) * chunk, width), F32),
             pltpu.VMEM((both, both), F32),
             pltpu.VMEM((16, width), F32),
             pltpu.VMEM((STEPS, row_count, width + 16, width), F32),
@@ -386,7 +424,7 @@
             dma((chunks,)), dma((chunks,)), dma((chunks,)), dma((chunks,)),
             dma((STEPS, row_count)), dma((STEPS, row_count)),
             dma((blk_count,)), dma((blk_count,)),
-            dma((2 + STEPS,)), dma((2 + STEPS,)),
+            dma((5 + STEPS,)), dma((5 + STEPS,)),
         ],
         compiler_params=pltpu.CompilerParams(
             collective_id=0, has_side_effects=True, vmem_limit_bytes=48 * 1024 * 1024

time: 117 us -> 114 us (0.974)
  Pallas kernels: 113 us -> 111 us
    pallas_call x1, Pallas kernels: 113 us -> 111 us  [on_device(): pl.pallas_call(functools.partial(kernel, row_count, blk_count, chunk, gra...]
where the time goes in v4:
time: 114 us
  Pallas kernels  111 us (97%)
  local copies, waits for them, and re-layouts  2.53 us (2%)
    pallas_call x1, Pallas kernels, on_device(): pl.pallas_call(functools.partial(kernel, row_count, blk_count, chunk, gra...  111 us
    unnamed x2, local copies, waits for them, and re-layouts  2.53 us

profile of v4, /device:TPU:0, one launch (start us, length us, event | category | flops | bytes accessed | tf_op | source)
XLA Modules:
  0.0 113.9 jit_solution(1784587747887865897)
XLA Ops:
  0.6 110.7 %shard_map.30 = (f32[4096,256]{1,0:T(8,128)S(1)}, f32[2]{0:T(128)S(1)}) custom-call(f32[4096,256]{1,0:T(8,128)} %x_hbm.1), custom_call_target="tpu_custom_call" | custom-call | tf_op jit(solution)/shard_map/pallas_call | solution.py:398
  111.4 2.0 %copy.5 = f32[4096,256]{1,0:T(8,128)} copy(f32[4096,256]{1,0:T(8,128)S(1)} %get-tuple-element.4) | data formatting | bytes 8388608
  113.4 0.5 copy.6

commit v5 on v4

--- a/solution.py
+++ b/solution.py
@@ -71,9 +71,9 @@
 
 
 def kernel(
-    row_count, blk_count, chunk, gram_chunk, early, given,
+    row_count, blk_count, chunk, gram_chunk, early, given, direct,
     x_hbm, out_ref, off_ref,
-    xv, move0, stay0, come0, move1, raw, rest, skip, hold,
+    xv, move0, stay0, come0, move1, raw, rest, skip, hold, lent,
     acc, norms, gath, weights, coses, cosin, measure, mgath,
     load_sem, send0, recv0, send1, recv1, gsend, grecv, msend, mrecv, esend, erecv,
 ):
@@ -127,6 +127,9 @@
     skip_move = ahead(move0.at[pl.ds(0, given * chunk)], skip, 1, second)
     give_move = ahead(stay0.at[given_rows], rest.at[given_rows], 2 + STEPS, after)
     hold_move = ahead(stay0.at[given_rows], hold, 3 + STEPS, below)
+    late_rows = pl.ds(given * chunk, (direct - given) * chunk)
+    lend_move = ahead(move1.at[late_rows], lent, 5 + STEPS, below)
+    land_move = ahead(lent, out_ref.at[late_rows, pl.ds(width, width)], 6 + STEPS, second)
     pass_move = ahead(hold, rest.at[given_rows], 2 + STEPS, second, 4 + STEPS)
     cos_moves = [ahead(coses.at[s], cosin.at[s], 2 + s, after) for s in range(STEPS)]
 
@@ -302,10 +305,14 @@
         out_ref[part, 0:width] = mixed[:, :width]
         move1[part] = mixed[:, width:]
 
-        @pl.when(i > given)
+        @pl.when(jnp.logical_or(i > direct, jnp.logical_and(i > given, jnp.logical_not(odd))))
         def _():
             second_move(i - 1).start()
 
+        @pl.when(jnp.logical_and(i == direct, odd))
+        def _():
+            lend_move.start()
+
         return carry
 
     lax.fori_loop(given, chunks, turn1, 0)
@@ -315,6 +322,8 @@
     def _():
         hold_move.wait_recv()
         pass_move.start()
+        lend_move.wait_recv()
+        land_move.start()
 
 
     def own1(i, carry):
@@ -363,7 +372,26 @@
         return carry
 
     lax.fori_loop(early, chunks, sent, 0)
-    lax.fori_loop(given, chunks, finish, 0)
+    lax.fori_loop(direct, chunks, finish, 0)
+
+    @pl.when(odd)
+    def _():
+        def arrived(i, carry):
+            second_move(i).wait_recv()
+            return carry
+
+        lax.fori_loop(given, direct, arrived, 0)
+        lend_move.wait_send()
+
+    @pl.when(jnp.logical_not(odd))
+    def _():
+        def left(i, carry):
+            second_move(i).wait_send()
+            return carry
+
+        lax.fori_loop(given, direct, left, 0)
+        land_move.wait_send()
+        land_move.wait_recv()
 
     @pl.when(odd)
     def _():
@@ -389,14 +417,14 @@
 def on_device(row_count, blk_count, matrix):
     rows, both = matrix.shape
     width = both // 2
-    chunks, early, given = 16, 2, 4
+    chunks, early, given, direct = 16, 3, 5, 7
     chunk = rows // chunks
     gram_chunk = rows // 8
     dma = pltpu.SemaphoreType.DMA
     block = pltpu.VMEM((rows, width), F32)
     some = pltpu.VMEM((given * chunk, width), F32)
     return pl.pallas_call(
-        functools.partial(kernel, row_count, blk_count, chunk, gram_chunk, early, given),
+        functools.partial(kernel, row_count, blk_count, chunk, gram_chunk, early, given, direct),
         out_shape=(
             jax.ShapeDtypeStruct((rows, both), F32),
             jax.ShapeDtypeStruct((STEPS,), F32),
@@ -412,6 +440,7 @@
             pltpu.VMEM((early * chunk, both), F32),
             some, some,
             pltpu.VMEM(((given - early) * chunk, width), F32),
+            pltpu.VMEM(((direct - given) * chunk, width), F32),
             pltpu.VMEM((both, both), F32),
             pltpu.VMEM((16, width), F32),
             pltpu.VMEM((STEPS, row_count, width + 16, width), F32),
@@ -424,7 +453,7 @@
             dma((chunks,)), dma((chunks,)), dma((chunks,)), dma((chunks,)),
             dma((STEPS, row_count)), dma((STEPS, row_count)),
             dma((blk_count,)), dma((blk_count,)),
-            dma((5 + STEPS,)), dma((5 + STEPS,)),
+            dma((7 + STEPS,)), dma((7 + STEPS,)),
         ],
         compiler_params=pltpu.CompilerParams(
             collective_id=0, has_side_effects=True, vmem_limit_bytes=48 * 1024 * 1024

time: 114 us -> 111 us (0.974)
  Pallas kernels: 111 us -> 108 us
    pallas_call x1, Pallas kernels: 111 us -> 108 us  [on_device(): pl.pallas_call(functools.partial(kernel, row_count, blk_count, chunk, gra...]
where the time goes in v5:
time: 111 us
  Pallas kernels  108 us (97%)
  local copies, waits for them, and re-layouts  2.53 us (2%)
    pallas_call x1, Pallas kernels, on_device(): pl.pallas_call(functools.partial(kernel, row_count, blk_count, chunk, gra...  108 us
    unnamed x2, local copies, waits for them, and re-layouts  2.53 us

profile of v5, /device:TPU:0, one launch (start us, length us, event | category | flops | bytes accessed | tf_op | source)
XLA Modules:
  0.0 111.1 jit_solution(12041892841971895564)
XLA Ops:
  0.6 108.0 %shard_map.30 = (f32[4096,256]{1,0:T(8,128)S(1)}, f32[2]{0:T(128)S(1)}) custom-call(f32[4096,256]{1,0:T(8,128)} %x_hbm.1), custom_call_target="tpu_custom_call" | custom-call | tf_op jit(solution)/shard_map/pallas_call | solution.py:426
  108.6 2.0 %copy.5 = f32[4096,256]{1,0:T(8,128)} copy(f32[4096,256]{1,0:T(8,128)S(1)} %get-tuple-element.4) | data formatting | bytes 8388608
  110.6 0.5 copy.6
